TPU v7x, 32 devices: a whole 2x2x4 slice. The times are simulated.
32 devices in a mesh: groups: 1, ctx: 16 (over z, y, x), tp: 2 (over core).
Axes of the slice: x: 2, y: 2, z: 4, core: 2. Of those that a mesh axis runs over, the one named last changes fastest.
Arguments:
- queries: bfloat16 [4, 32, 64, 128], P('groups', 'ctx', 'tp'), may hold values from -100 to 100
- cand_keys: bfloat16 [4, 32, 8, 128], P('groups', 'ctx', 'tp'), may hold values from -4 to 4
- candidate_values: bfloat16 [4, 32, 8, 128], P('groups', 'ctx', 'tp'), may hold values from -5 to 5
- cached_prompt_keys: bfloat16 [256, 128, 8, 128], P(('groups', 'ctx'), None, 'tp'), may hold values from -4 to 4
- cached_prompt_values: bfloat16 [256, 128, 8, 128], P(('groups', 'ctx'), None, 'tp'), may hold values from -5 to 5
- block_lists: int32 [4, 128], P('groups'), may hold values from 0 to 255, as said below
- out_weight: bfloat16 [8192, 8192], P('tp', 'ctx'), may hold values from -0.0625 to 0.0625
Outputs:
- verified: bfloat16 [4, 32, 8192], P('groups', 'tp', 'ctx')
Inputs may be any that keep to these rules, and one draw needn't show every extreme that they name: `block_lists`: each row holds 128 distinct block numbers in increasing order; among blocks 16 * c to 16 * (c + 1) - 1 a row has at most 16 entries, exactly 16 for some c in every row; all rows together have at most 40 entries in one such range, exactly 40 in some.
All inputs are finite; a program needn't handle non-finite values.
Results may differ from a plain program's by a relative error of at most 0.022.
Values may be sent and summed in bfloat16 or wider, within the bound.
A program may use at most 128 MiB of HBM per device.

v0:
```python
import jax
import jax.numpy as jnp
from jax import lax
from jax.sharding import PartitionSpec as P

NEGATIVE = -1e30


def masked_softmax(scores, visible):
    scores = jnp.where(visible, scores, NEGATIVE)
    maxima = jnp.max(scores, axis=-1)
    weights = jnp.where(visible, jnp.exp(scores - maxima[..., None]), 0.0)
    return (weights, maxima, jnp.sum(weights, axis=-1))


def heads_last(stats):
    kv_count, query_group_width, row_count = stats.shape
    return jnp.transpose(stats, (2, 0, 1)).reshape(row_count, kv_count * query_group_width)


def block_terms(query_matrix, block_keys, block_values, visible, factor):
    row_count, kv_count, query_group_width, head_size = query_matrix.shape
    scores = (
        jnp.einsum("nkgd,mkd->kgnm", query_matrix, block_keys, preferred_element_type=jnp.float32)
        * factor
    )
    weights, maxima, denominator = masked_softmax(scores, visible)
    numerator = jnp.einsum(
        "kgnm,mkd->nkgd",
        weights.astype(jnp.bfloat16),
        block_values,
        preferred_element_type=jnp.float32,
    )
    return (
        numerator.reshape(row_count, kv_count * query_group_width, head_size),
        heads_last(maxima),
        heads_last(denominator),
    )


def join_parts(first, second):
    maxima = jnp.maximum(first[1], second[1])
    left_scale = jnp.exp(first[1] - maxima)
    right_scale = jnp.exp(second[1] - maxima)
    numerator = first[0] * left_scale[..., None] + second[0] * right_scale[..., None]
    return (numerator, maxima, first[2] * left_scale + second[2] * right_scale)


def sources_merge(parts):
    numerator, maxima, denominator = parts
    highest = jnp.max(maxima, axis=2)
    rescale = jnp.exp(maxima - highest[:, :, None])
    return (
        jnp.sum(numerator * rescale[..., None], axis=2),
        highest,
        jnp.sum(denominator * rescale, axis=2),
    )


def on_device(
    queries,
    cand_keys,
    candidate_values,
    cached_prompt_keys,
    cached_prompt_values,
    block_lists,
    out_weight,
):
    cand_count, tok_rows, head_local, head_size = queries.shape
    kv_local = cand_keys.shape[2]
    query_group_width = head_local // kv_local
    blocks_here, block_tokens = (cached_prompt_keys.shape[0], cached_prompt_keys.shape[1])
    selected = block_lists.shape[1]
    ranges = lax.axis_size("ctx")
    device = lax.axis_index("ctx")
    cand_length = tok_rows * ranges
    factor = head_size ** (-0.5)
    capacity = min(blocks_here, 4 * selected // ranges)
    lowest = device * blocks_here
    below = jnp.sum((block_lists < lowest).astype(jnp.int32), axis=1)
    inside = jnp.sum((block_lists < lowest + blocks_here).astype(jnp.int32), axis=1) - below
    slot_ids = jnp.arange(capacity)
    where_listed = jnp.clip(below[:, None] + slot_ids[None, :], 0, selected - 1)
    slot_live = slot_ids[None, :] < inside[:, None]
    local_index = jnp.where(
        slot_live, jnp.take_along_axis(block_lists, where_listed, axis=1) - lowest, 0
    )
    gathered_keys = jnp.take(cached_prompt_keys, local_index, axis=0).reshape(
        cand_count, capacity * block_tokens, kv_local, head_size
    )
    gathered_values = jnp.take(cached_prompt_values, local_index, axis=0).reshape(
        cand_count, capacity * block_tokens, kv_local, head_size
    )
    key_live = jnp.repeat(slot_live, block_tokens, axis=1)
    shard_rows = lax.all_gather(queries, "ctx", axis=1, tiled=True)
    row_count = shard_rows.shape[1]
    grouped_queries = shard_rows.reshape(
        cand_count, row_count, kv_local, query_group_width, head_size
    )
    terms = lax.map(
        lambda parts: block_terms(parts[0], parts[1], parts[2], parts[3], factor),
        (grouped_queries, gathered_keys, gathered_values, key_live),
    )
    prompt_parts = tuple((fresh for fresh in terms))
    candidate_own_keys, own_values = (
        lax.all_gather(cand_keys, "ctx", axis=1, tiled=True),
        lax.all_gather(candidate_values, "ctx", axis=1, tiled=True),
    )
    query_pos = device * tok_rows + jnp.arange(tok_rows)
    causal = jnp.arange(cand_length)[None, :] <= query_pos[:, None]
    grouped_local = queries.reshape(cand_count, tok_rows, kv_local, query_group_width, head_size)
    own_scores = (
        jnp.einsum(
            "jnkgd,jmkd->jkgnm",
            grouped_local,
            candidate_own_keys,
            preferred_element_type=jnp.float32,
        )
        * factor
    )
    own_weights, own_max, own_sum = masked_softmax(own_scores, causal)
    own_numer = jnp.einsum(
        "jkgnm,jmkd->jnkgd",
        own_weights.astype(jnp.bfloat16),
        own_values,
        preferred_element_type=jnp.float32,
    )
    own_part = (
        own_numer.reshape(cand_count, tok_rows, head_local, head_size),
        jnp.transpose(own_max, (0, 3, 1, 2)).reshape(cand_count, tok_rows, head_local),
        jnp.transpose(own_sum, (0, 3, 1, 2)).reshape(cand_count, tok_rows, head_local),
    )
    merged = sources_merge(
        (
            lax.all_to_all(
                prompt_parts[0][:, :, None].astype(jnp.bfloat16),
                "ctx",
                split_axis=1,
                concat_axis=2,
                tiled=True,
            ).astype(jnp.float32),
            lax.all_to_all(
                prompt_parts[1][:, :, None].astype(jnp.bfloat16),
                "ctx",
                split_axis=1,
                concat_axis=2,
                tiled=True,
            ).astype(jnp.float32),
            lax.all_to_all(
                prompt_parts[2][:, :, None].astype(jnp.bfloat16),
                "ctx",
                split_axis=1,
                concat_axis=2,
                tiled=True,
            ).astype(jnp.float32),
        )
    )
    numerator, unused_max, denominator = join_parts(merged, own_part)
    attention = (
        (numerator / denominator[..., None])
        .reshape(cand_count, tok_rows, head_local * head_size)
        .astype(jnp.bfloat16)
    )
    partial_value = jnp.einsum(
        "jnf,fc->jnc",
        lax.all_gather(attention, "ctx", axis=1, tiled=True),
        out_weight,
        preferred_element_type=jnp.float32,
    )
    return lax.psum_scatter(
        partial_value.astype(jnp.bfloat16), "tp", scatter_dimension=1, tiled=True
    )


def solution(mesh):
    placed = (
        P("groups", "ctx", "tp", None),
        P("groups", "ctx", "tp", None),
        P("groups", "ctx", "tp", None),
        P(("groups", "ctx"), None, "tp", None),
        P(("groups", "ctx"), None, "tp", None),
        P("groups", None),
        P("tp", "ctx"),
    )
    return jax.shard_map(
        on_device, mesh=mesh, in_specs=placed, out_specs=P("groups", "tp", "ctx"), check_vma=False
    )
```

profile of v0, /device:TPU:0, one launch (start us, length us, event | category | flops | bytes accessed | tf_op | source)
XLA Modules:
  0.0 323.0 jit_solution(12083824224312323788)
XLA Ops:
  6.5 0.7 all-gather.3.cloned.1.call-update
  7.3 0.8 convert_reduce_fusion.1
  8.3 1.6 gather_fusion
  9.9 0.1 reshape.205
  10.1 9.3 %gather_fusion.1 = bf16[64,128,4,128]{3,2,1,0:T(4,128)(2,1)} fusion(bf16[16,128,4,128]{3,2,1,0:T(4,128)(2,1)S(1)} %copy-done, s32[1024]{0:T(1024)S(1)} %pad_clamp_fusion), kind=kCustom, calls=%fused_computation.clone | custom fusion | bytes 16777472 | tf_op jit(solution)/shard_map/jit(_take)/gather | solution.py:91
  19.4 10.9 %gather_fusion.2 = bf16[64,128,4,128]{3,2,1,0:T(4,128)(2,1)} fusion(bf16[16,128,4,128]{3,2,1,0:T(4,128)(2,1)} %param.14, s32[1024]{0:T(1024)S(1)} %pad_clamp_fusion), kind=kCustom, calls=%fused_computation.1.clone | custom fusion | bytes 16777472 | tf_op jit(solution)/shard_map/jit(_take)/gather | solution.py:88
  30.5 14.7 %copy_select_fusion = (bf16[4,16,128,4,128]{4,2,1,3,0:T(8,128)(2,1)}, bf16[4,16,128,4,128]{4,2,1,3,0:T(8,128)(2,1)}) fusion(bf16[4,16,128,4,128]{4,3,2,1,0:T(4,128)(2,1)} %bitcast.150, pred[4,16]{1,0:T(4,128)(4,1)S(1)} %get-tuple-element.82, bf16[4,16,128,4,128]{4,3,2,1,0:T(4,128)(2,1)} %bitcast.149), kind=kLoop, calls=%fused_computation.27 | loop fusion | flops 8388608 | bytes 33554496 | tf_op jit(solution)/shard_map/jit(_take)/select_n | solution.py:88
  45.1 22.6 %all-gather.3.cloned.1.call-done = bf16[4,32,32,128]{3,2,1,0:T(8,128)(2,1)} async-done(((bf16[4,2,32,128]{3,2,1,0:T(8,128)(2,1)}), bf16[4,32,32,128]{3,2,1,0:T(8,128)(2,1)}) %all-gather.3.cloned.1.call-update) | async-done | bytes 1048592 | tf_op jit(solution)/shard_map/all_gather | solution.py:95
  67.8 1.6 copy.71
  69.4 61.6 %while.14 = (s32[]{:T(128)}, bf16[4,32,32,128]{3,2,0,1:T(8,128)(2,1)}, bf16[4,32,32]{2,0,1:T(4,128)(2,1)S(1)}, bf16[4,32,32]{2,0,1:T(4,128)(2,1)S(1)}, bf16[4,20...) while((s32[]{:T(128)}, ...), condition=%wide.region_5.7_spmd, body=%wide.region_2.6_spmd.sunk | while | flops 1101002752 | bytes 64022668 | solution.py:100
  69.5 3.0 bitcast_reduce_fusion.2
  72.5 3.2 copy-done.1
  75.7 2.2 fusion.59
  77.9 0.1 copy.132
  78.0 0.1 dynamic_update_slice.17
  78.1 5.7 %fusion.58 = bf16[4,128,8,32]{1,3,2,0:T(8,128)(2,1)S(1)} fusion(f32[4,2048,32,8]{1,2,3,0:T(8,128)} %copy-done.1, f32[4,8,32]{2,1,0:T(8,128)S(1)} %get-tuple-element.148, pred[2048]{0:T(1024)(128)(4,1)S(1)} %dynamic-slice_reduce_fusion.2, bf16[4,2048,4,128]{3,1,2,0:T(8,128)(2,1)} %get-tuple-element.173, s32[]{:T(128)} %get-tuple-element.159), kind=kOutput, calls=%fused_computation.10.clone.1 | convolution fusion | flops 547356672 | bytes 10768896 | tf_op jit(solution)/shard_map/while/body/eval_jaxpr/kgnm,mkd->nkgd/dot_general | solution.py:28
  83.8 0.9 copy_dynamic-update-slice_fusion.2
  84.9 3.0 bitcast_reduce_fusion.2
  87.9 3.2 copy-done.1
  91.1 2.2 fusion.59
  93.3 0.1 copy.132
  93.4 0.1 dynamic_update_slice.17
  93.5 5.7 %fusion.58 = bf16[4,128,8,32]{1,3,2,0:T(8,128)(2,1)S(1)} fusion(f32[4,2048,32,8]{1,2,3,0:T(8,128)} %copy-done.1, f32[4,8,32]{2,1,0:T(8,128)S(1)} %get-tuple-element.148, pred[2048]{0:T(1024)(128)(4,1)S(1)} %dynamic-slice_reduce_fusion.2, bf16[4,2048,4,128]{3,1,2,0:T(8,128)(2,1)} %get-tuple-element.173, s32[]{:T(128)} %get-tuple-element.159), kind=kOutput, calls=%fused_computation.10.clone.1 | convolution fusion | flops 547356672 | bytes 10768896 | tf_op jit(solution)/shard_map/while/body/eval_jaxpr/kgnm,mkd->nkgd/dot_general | solution.py:28
  99.2 0.9 copy_dynamic-update-slice_fusion.2
  100.3 3.0 bitcast_reduce_fusion.2
  103.3 3.2 copy-done.1
  106.5 2.2 fusion.59
  108.7 0.1 copy.132
  108.8 0.1 dynamic_update_slice.17
  108.9 5.7 %fusion.58 = bf16[4,128,8,32]{1,3,2,0:T(8,128)(2,1)S(1)} fusion(f32[4,2048,32,8]{1,2,3,0:T(8,128)} %copy-done.1, f32[4,8,32]{2,1,0:T(8,128)S(1)} %get-tuple-element.148, pred[2048]{0:T(1024)(128)(4,1)S(1)} %dynamic-slice_reduce_fusion.2, bf16[4,2048,4,128]{3,1,2,0:T(8,128)(2,1)} %get-tuple-element.173, s32[]{:T(128)} %get-tuple-element.159), kind=kOutput, calls=%fused_computation.10.clone.1 | convolution fusion | flops 547356672 | bytes 10768896 | tf_op jit(solution)/shard_map/while/body/eval_jaxpr/kgnm,mkd->nkgd/dot_general | solution.py:28
  114.6 0.9 copy_dynamic-update-slice_fusion.2
  115.7 3.0 bitcast_reduce_fusion.2
  118.7 3.2 copy-done.1
  121.9 2.2 fusion.59
  124.1 0.1 copy.132
  124.2 0.1 dynamic_update_slice.17
  124.3 5.7 %fusion.58 = bf16[4,128,8,32]{1,3,2,0:T(8,128)(2,1)S(1)} fusion(f32[4,2048,32,8]{1,2,3,0:T(8,128)} %copy-done.1, f32[4,8,32]{2,1,0:T(8,128)S(1)} %get-tuple-element.148, pred[2048]{0:T(1024)(128)(4,1)S(1)} %dynamic-slice_reduce_fusion.2, bf16[4,2048,4,128]{3,1,2,0:T(8,128)(2,1)} %get-tuple-element.173, s32[]{:T(128)} %get-tuple-element.159), kind=kOutput, calls=%fused_computation.10.clone.1 | convolution fusion | flops 547356672 | bytes 10768896 | tf_op jit(solution)/shard_map/while/body/eval_jaxpr/kgnm,mkd->nkgd/dot_general | solution.py:28
  130.0 0.8 copy_dynamic-update-slice_fusion.2
  131.1 0.7 reshape.228
  131.8 4.5 %all-to-all-start.2 = ((bf16[16,2,128]{2,1,0:T(2,128)(2,1)}), bf16[16,2,128]{2,1,0:T(2,128)(2,1)S(1)}, u32[]{:S(2)}, u32[]{:S(2)}) async-start(bf16[16,2,128]{2,1,0:T(2,128)(2,1)} %reshape.228), calls=%async_computation.2 | async-start | bytes 16384 | tf_op jit(solution)/shard_map/all_to_all | solution.py:149
  136.3 0.1 reshape.226
  136.4 7.1 %all-to-all-done.2 = bf16[16,2,128]{2,1,0:T(2,128)(2,1)S(1)} async-done(((bf16[16,2,128]{2,1,0:T(2,128)(2,1)}), bf16[16,2,128]{2,1,0:T(2,128)(2,1)S(1)}, u32[]{:S(2)}, u32[]{:S(2)}) %all-to-all-start.2) | async-done | bytes 8224 | tf_op jit(solution)/shard_map/all_to_all | solution.py:149
  143.5 9.9 %all_to_all.33 = bf16[16,2,128]{2,1,0:T(2,128)(2,1)S(1)} all-to-all(bf16[16,2,128]{2,1,0:T(2,128)(2,1)S(1)} %reshape.226), channel_id=1, replica_groups=mesh['groups'=1,'ctx'=16,'tp'=2] {'ctx'}, dimensions={0} | all-to-all | bytes 16384 | tf_op jit(solution)/shard_map/all_to_all | solution.py:142
  153.4 3.7 %all-to-all-start = ((bf16[4,32,1,32,128]{4,3,0,2,1:T(8,128)(2,1)}), bf16[4,32,1,32,128]{4,3,0,2,1:T(8,128)(2,1)S(1)}, u32[]{:S(2)}, u32[]{:S(2)}) async-start(bf16[4,32,1,32,128]{4,3,0,2,1:T(8,128)(2,1)} %bitcast.156), calls=%async_computation | async-start | bytes 2097152 | tf_op jit(solution)/shard_map/all_to_all | solution.py:135
  157.1 47.7 %all_gather.13 = bf16[4,32,4,128]{3,2,0,1:T(4,128)(2,1)S(1)} all-gather(bf16[4,2,4,128]{3,2,0,1:T(4,128)(2,1)S(1)} %copy.77), channel_id=1, replica_groups=mesh['groups'=1,'ctx'=16,'tp'=2] {'ctx'}, dimensions={1}, use_global_device_ids=true | all-gather | bytes 139264 | tf_op jit(solution)/shard_map/all_gather | solution.py:106
  204.8 0.3 fusion.50
  205.1 0.2 fusion.33
  205.4 0.1 reshape.180
  205.5 0.1 reshape.178
  205.6 38.1 %all_gather.14 = bf16[4,32,4,128]{3,2,0,1:T(4,128)(2,1)S(1)} all-gather(bf16[4,2,4,128]{3,2,0,1:T(4,128)(2,1)S(1)} %copy.82), channel_id=1, replica_groups=mesh['groups'=1,'ctx'=16,'tp'=2] {'ctx'}, dimensions={1}, use_global_device_ids=true | all-gather | bytes 139264 | tf_op jit(solution)/shard_map/all_gather | solution.py:107
  243.7 0.2 convolution_bitcast_fusion
  244.0 0.1 reshape.229
  244.3 1.5 copy.76
  245.8 0.1 div.11
  246.0 0.7 mul.77
  246.7 1.0 mul.78
  247.7 0.7 copy.81
  248.4 0.3 convert.23
  248.7 3.9 %fusion.22 = f32[4,2,32,128]{3,1,2,0:T(2,128)S(1)} fusion(f32[4,16,2,1,32,128]{5,4,0,2,1,3:T(8,128)S(1)} %convert.23, f32[4,2,16,32]{1,2,3,0:T(8,128)} %copy.76), kind=kLoop, calls=%fused_computation.32 | loop fusion | flops 1015808 | bytes 2244608 | tf_op jit(solution)/shard_map/reduce_sum | solution.py:54
  252.6 1.1 fusion.32
  253.7 0.7 copy.88
  254.4 51.1 %all-gather.5.cloned.1.call-done = bf16[4,32,4096]{2,0,1:T(4,128)(2,1)} async-done(((bf16[4,2,4096]{2,0,1:T(4,128)(2,1)}), bf16[4,32,4096]{2,0,1:T(4,128)(2,1)}) %all-gather.5.cloned.1.call-update) | async-done | bytes 1048592 | tf_op jit(solution)/shard_map/all_gather | solution.py:166
  305.5 4.4 %fusion.23 = bf16[4,32,512]{2,1,0:T(8,128)(2,1)} fusion(bf16[4096,512]{1,0:T(8,128)(2,1)} %param.17, bf16[4,32,4096]{2,0,1:T(4,128)(2,1)} %all-gather.5.cloned.1.call-done), kind=kOutput, calls=%fused_computation.33 | convolution fusion | flops 536936448 | bytes 5373952 | tf_op jit(solution)/shard_map/jnf,fc->jnc/dot_general | solution.py:164
  309.9 6.6 %reduce-scatter.2.cloned.1.call-done = bf16[4,16,512]{2,1,0:T(8,128)(2,1)} async-done(((bf16[4,32,512]{2,1,0:T(8,128)(2,1)}), bf16[4,16,512]{2,1,0:T(8,128)(2,1)}) %reduce-scatter.2.cloned.1.call-update) | async-done | bytes 65552 | tf_op jit(solution)/shard_map/reduce_scatter | solution.py:170
  (59 shorter events, 1.9 us)
Async XLA Ops:
  6.5 3.6 %copy-start = (bf16[16,128,4,128]{3,2,1,0:T(4,128)(2,1)S(1)}, bf16[16,128,4,128]{3,2,1,0:T(4,128)(2,1)}, u32[]{:S(2)}) copy-start(bf16[16,128,4,128]{3,2,1,0:T(4,128)(2,1)} %param.15) | copy-start | bytes 6291460
  6.5 61.2 %all-gather.3.cloned.1.call-start = ((), (), s32[]{:S(2)}) async-start(), calls=%async_computation.4 | async-start | bytes 1114112 | tf_op jit(solution)/shard_map/all_gather | solution.py:95
  69.4 87.7 %copy-start.3 = (bf16[4,2,4,128]{3,2,1,0:T(4,128)(2,1)S(1)}, bf16[4,2,4,128]{3,2,1,0:T(4,128)(2,1)}, u32[]{:S(2)}) copy-start(bf16[4,2,4,128]{3,2,1,0:T(4,128)(2,1)} %param.12) | copy-start | bytes 24580
  69.4 135.4 %copy-start.2 = (bf16[4,2,32,128]{3,2,1,0:T(8,128)(2,1)S(1)}, bf16[4,2,32,128]{3,2,1,0:T(8,128)(2,1)}, u32[]{:S(2)}) copy-start(bf16[4,2,32,128]{3,2,1,0:T(8,128)(2,1)} %param.11) | copy-start | bytes 196612
  69.4 136.1 %copy-start.4 = (bf16[4,2,4,128]{3,2,1,0:T(4,128)(2,1)S(1)}, bf16[4,2,4,128]{3,2,1,0:T(4,128)(2,1)}, u32[]{:S(2)}) copy-start(bf16[4,2,4,128]{3,2,1,0:T(4,128)(2,1)} %param.13) | copy-start | bytes 24580
  72.5 3.2 copy-start.1
  87.9 3.2 copy-start.1
  103.3 3.2 copy-start.1
  118.7 3.2 copy-start.1
  131.8 11.7 %all-to-all-start.2 = ((bf16[16,2,128]{2,1,0:T(2,128)(2,1)}), bf16[16,2,128]{2,1,0:T(2,128)(2,1)S(1)}, u32[]{:S(2)}, u32[]{:S(2)}) async-start(bf16[16,2,128]{2,1,0:T(2,128)(2,1)} %reshape.228), calls=%async_computation.2 | async-start | bytes 16384 | tf_op jit(solution)/shard_map/all_to_all | solution.py:149
  153.4 95.1 %all-to-all-start = ((bf16[4,32,1,32,128]{4,3,0,2,1:T(8,128)(2,1)}), bf16[4,32,1,32,128]{4,3,0,2,1:T(8,128)(2,1)S(1)}, u32[]{:S(2)}, u32[]{:S(2)}) async-start(bf16[4,32,1,32,128]{4,3,0,2,1:T(8,128)(2,1)} %bitcast.156), calls=%async_computation | async-start | bytes 2097152 | tf_op jit(solution)/shard_map/all_to_all | solution.py:135
  157.0 148.5 %all-gather.5.cloned.1.call-start = ((), (), s32[]{:S(2)}) async-start(), calls=%async_computation.5 | async-start | bytes 1114112 | tf_op jit(solution)/shard_map/all_gather | solution.py:166
  254.4 62.1 %reduce-scatter.2.cloned.1.call-start = ((), (), s32[]{:S(2)}) async-start(), calls=%async_computation.6 | async-start | bytes 196608 | tf_op jit(solution)/shard_map/reduce_scatter | solution.py:170
Sparse Core Ops, SparseCore 0:
  10.1 57.6 all-gather.2
  254.5 50.9 all-gather.4
  310.0 6.4 reduce-scatter.1
where the time goes:
time: 324 us; the launch traced here: 323 us
  blocking collectives  95.6 us (30%)
  waiting for transfers between devices  88.1 us (27%)
  local copies, waits for them, and re-layouts  47.6 us (15%)
  matrix products  39.7 us (12%)
  other arithmetic  30.1 us (9%)
  between operations  13.4 us (4%)
  starting transfers between devices  8.24 us (3%)
    all_gather x1, waiting for transfers between devices, on_device(): lax.all_gather(attention, 'ctx', axis=1, tiled=True)  51.1 us
    all_gather x1, blocking collectives, on_device(): lax.all_gather(cand_keys, 'ctx', axis=1, tiled=True)  47.7 us
    all_gather x1, blocking collectives, on_device(): lax.all_gather(candidate_values, 'ctx', axis=1, tiled=True)  38.1 us
    dot_general x4, matrix products, block_terms(): jnp.einsum('kgnm,mkd->nkgd', weights.astype(jnp.bfloat16), block_values,...  22.9 us
    all_gather x1, waiting for transfers between devices, on_device(): shard_rows = lax.all_gather(queries, 'ctx', axis=1, tiled=True)  22.6 us
    select_n x1, other arithmetic, on_device(): jnp.take(cached_prompt_keys, local_index, axis=0)  14.7 us
    while x8, local copies, waits for them, and re-layouts  12.9 us
    dot_general x4, matrix products, block_terms(): jnp.einsum('nkgd,mkd->kgnm', query_matrix, block_keys, preferred_element_...  12 us
  transfers between devices with their start and end apart: 5, of which 4 were waited for; matrix products, arithmetic and copies ran while one was open for 13% of the time, Pallas kernels for 0%

commit v1 on v0

--- a/solution.py
+++ b/solution.py
@@ -4,6 +4,31 @@
 from jax.sharding import PartitionSpec as P
 
 NEGATIVE = -1e30
+
+
+def state_surface(tile_in, frame):
+    odd = lax.axis_size("ctx")
+    f_next = lax.axis_index("ctx")
+    lower, tmp, u1 = (odd, f_next, tile_in.shape[1])
+    u_next, step_out = ([], [])
+    built = d_next = tile_in
+    num = 0
+    while num < lower // 2 + 1:
+        everything = frame(built, (tmp - num) % lower * u1)
+        u_next.append(everything)
+        if 0 < num < lower - lower // 2:
+            opened = frame(d_next, (tmp + num) % lower * u1)
+            step_out.append(opened)
+        built = lax.ppermute(
+            built, axis_name="ctx", perm=[(dev, (dev + 1) % lower) for dev in range(lower)]
+        )
+        d_next = lax.ppermute(
+            d_next, axis_name="ctx", perm=[(dev, (dev - 1) % lower) for dev in range(lower)]
+        )
+        num = num + 1
+    row_out = jnp.concatenate([*u_next[::-1], *step_out], axis=1)
+    mid_arr = jnp.roll(row_out, (tmp - lower // 2) * u_next[0].shape[1], axis=1)
+    return mid_arr
 
 
 def masked_softmax(scores, visible):
@@ -161,11 +186,11 @@
         .reshape(cand_count, tok_rows, head_local * head_size)
         .astype(jnp.bfloat16)
     )
-    partial_value = jnp.einsum(
-        "jnf,fc->jnc",
-        lax.all_gather(attention, "ctx", axis=1, tiled=True),
-        out_weight,
-        preferred_element_type=jnp.float32,
+    partial_value = state_surface(
+        attention,
+        frame=lambda own_block, start: jnp.einsum(
+            "jnf,fc->jnc", own_block, out_weight, preferred_element_type=jnp.float32
+        ),
     )
     return lax.psum_scatter(
         partial_value.astype(jnp.bfloat16), "tp", scatter_dimension=1, tiled=True

time: 324 us -> 344 us (1.062)
  starting transfers between devices: 8.24 us -> 47.8 us
  waiting for transfers between devices: 88.1 us -> 66.7 us
  matrix products: 39.7 us -> 48.6 us
  local copies, waits for them, and re-layouts: 47.6 us -> 40.3 us
    all_gather x1 -> x0, waiting for transfers between devices: 51.1 us -> none  [on_device(): lax.all_gather(attention, 'ctx', axis=1, tiled=True)]
    ppermute x0 -> x15, starting transfers between devices: none -> 39.6 us  [the longest x7 39.3 us: state_surface(): lax.ppermute(d_next, axis_name='ctx', perm=[(dev, (dev - 1) % lower) for...]
    ppermute x0 -> x15, waiting for transfers between devices: none -> 23.6 us  [the longest x8 23.6 us: state_surface(): lax.ppermute(built, axis_name='ctx', perm=[(dev, (dev + 1) % lower) for d...]
    unnamed x3, waiting for transfers between devices: 0.74 us -> 13.4 us
    dot_general x1 -> x16, matrix products: 4.37 us -> 13.3 us  [on_device(): jnp.einsum('jnf,fc->jnc', own_block, out_weight, preferred_element_type=j...]
    while x8, local copies, waits for them, and re-layouts: 12.9 us -> 4.18 us
    reduce_scatter x1 -> x0, waiting for transfers between devices: 6.57 us -> none  [on_device(): lax.psum_scatter(partial_value.astype(jnp.bfloat16), 'tp', scatter_dimens...]
  transfers between devices with their start and end apart: 5 -> 19, of which waited for: 4 -> 11; matrix products, arithmetic and copies ran while one was open for 13% -> 16% of each run, Pallas kernels for 0% -> 0%
where the time goes in v1:
time: 344 us; the launch traced here: 343 us
  blocking collectives  95.6 us (28%)
  waiting for transfers between devices  66.7 us (19%)
  matrix products  48.6 us (14%)
  starting transfers between devices  47.8 us (14%)
  local copies, waits for them, and re-layouts  40.3 us (12%)
  other arithmetic  29.4 us (9%)
  between operations  14.6 us (4%)
    all_gather x1, blocking collectives, on_device(): lax.all_gather(cand_keys, 'ctx', axis=1, tiled=True)  47.7 us
    ppermute x7, starting transfers between devices, state_surface(): lax.ppermute(d_next, axis_name='ctx', perm=[(dev, (dev - 1) % lower) for...  39.3 us
    all_gather x1, blocking collectives, on_device(): lax.all_gather(candidate_values, 'ctx', axis=1, tiled=True)  38.1 us
    ppermute x8, waiting for transfers between devices, state_surface(): lax.ppermute(built, axis_name='ctx', perm=[(dev, (dev + 1) % lower) for d...  23.6 us
    dot_general x4, matrix products, block_terms(): jnp.einsum('kgnm,mkd->nkgd', weights.astype(jnp.bfloat16), block_values,...  22.8 us
    all_gather x1, waiting for transfers between devices, on_device(): shard_rows = lax.all_gather(queries, 'ctx', axis=1, tiled=True)  22.6 us
    select_n x1, other arithmetic, on_device(): jnp.take(cached_prompt_keys, local_index, axis=0)  14.7 us
    unnamed x3, waiting for transfers between devices  13.4 us
  transfers between devices with their start and end apart: 19, of which 11 were waited for; matrix products, arithmetic and copies ran while one was open for 16% of the time, Pallas kernels for 0%

profile of v1, /device:TPU:0, one launch (start us, length us, event | category | flops | bytes accessed | tf_op | source)
XLA Modules:
  0.0 343.3 jit_solution(12627621155889285662)
XLA Ops:
  6.5 0.7 all-gather.2.cloned.1.call-update
  7.3 0.8 convert_reduce_fusion.1
  8.3 1.6 gather_fusion
  10.1 9.3 %gather_fusion.1 = bf16[64,128,4,128]{3,2,1,0:T(4,128)(2,1)} fusion(bf16[16,128,4,128]{3,2,1,0:T(4,128)(2,1)S(1)} %copy-done, s32[1024]{0:T(1024)S(1)} %pad_clamp_fusion), kind=kCustom, calls=%fused_computation.clone | custom fusion | bytes 16777472 | tf_op jit(solution)/shard_map/jit(_take)/gather | solution.py:116
  19.4 11.0 %gather_fusion.2 = bf16[64,128,4,128]{3,2,1,0:T(4,128)(2,1)} fusion(bf16[16,128,4,128]{3,2,1,0:T(4,128)(2,1)} %param.14, s32[1024]{0:T(1024)S(1)} %pad_clamp_fusion), kind=kCustom, calls=%fused_computation.1.clone | custom fusion | bytes 16777472 | tf_op jit(solution)/shard_map/jit(_take)/gather | solution.py:113
  30.5 14.7 %copy_select_fusion = (bf16[4,16,128,4,128]{4,2,1,3,0:T(8,128)(2,1)}, bf16[4,16,128,4,128]{4,2,1,3,0:T(8,128)(2,1)}) fusion(bf16[4,16,128,4,128]{4,3,2,1,0:T(4,128)(2,1)} %bitcast.231, pred[4,16]{1,0:T(4,128)(4,1)S(1)} %get-tuple-element.82, bf16[4,16,128,4,128]{4,3,2,1,0:T(4,128)(2,1)} %bitcast.230), kind=kLoop, calls=%fused_computation.27 | loop fusion | flops 8388608 | bytes 33554496 | tf_op jit(solution)/shard_map/jit(_take)/select_n | solution.py:113
  45.2 22.6 %all-gather.2.cloned.1.call-done = bf16[4,32,32,128]{3,2,1,0:T(8,128)(2,1)} async-done(((bf16[4,2,32,128]{3,2,1,0:T(8,128)(2,1)}), bf16[4,32,32,128]{3,2,1,0:T(8,128)(2,1)}) %all-gather.2.cloned.1.call-update) | async-done | bytes 1048592 | tf_op jit(solution)/shard_map/all_gather | solution.py:120
  67.8 1.6 copy.84
  69.4 52.8 %while.14 = (s32[]{:T(128)}, bf16[4,32,32,128]{3,2,0,1:T(8,128)(2,1)}, bf16[4,32,32]{2,0,1:T(4,128)(2,1)S(1)}, bf16[4,32,32]{2,0,1:T(4,128)(2,1)S(1)}, bf16[4,20...) while((s32[]{:T(128)}, ...), condition=%wide.region_5.7_spmd, body=%wide.region_2.6_spmd.sunk | while | flops 1101002752 | bytes 64022668 | solution.py:125
  69.5 3.0 bitcast_reduce_fusion.2
  72.5 2.2 fusion.100
  74.7 1.0 copy-done.2
  75.9 5.7 %fusion.99 = bf16[4,128,8,32]{1,3,2,0:T(8,128)(2,1)S(1)} fusion(f32[4,2048,32,8]{1,2,3,0:T(8,128)} %copy-done.2, f32[4,8,32]{2,1,0:T(8,128)S(1)} %get-tuple-element.180, pred[2048]{0:T(1024)(128)(4,1)S(1)} %dynamic-slice_reduce_fusion.2, bf16[4,2048,4,128]{3,1,2,0:T(8,128)(2,1)} %get-tuple-element.205, s32[]{:T(128)} %get-tuple-element.191), kind=kOutput, calls=%fused_computation.10.clone.1 | convolution fusion | flops 547356672 | bytes 10768896 | tf_op jit(solution)/shard_map/while/body/eval_jaxpr/kgnm,mkd->nkgd/dot_general | solution.py:53
  81.6 0.8 copy_dynamic-update-slice_fusion.2
  82.7 3.0 bitcast_reduce_fusion.2
  85.7 2.2 fusion.100
  87.9 1.0 copy-done.2
  89.1 5.7 %fusion.99 = bf16[4,128,8,32]{1,3,2,0:T(8,128)(2,1)S(1)} fusion(f32[4,2048,32,8]{1,2,3,0:T(8,128)} %copy-done.2, f32[4,8,32]{2,1,0:T(8,128)S(1)} %get-tuple-element.180, pred[2048]{0:T(1024)(128)(4,1)S(1)} %dynamic-slice_reduce_fusion.2, bf16[4,2048,4,128]{3,1,2,0:T(8,128)(2,1)} %get-tuple-element.205, s32[]{:T(128)} %get-tuple-element.191), kind=kOutput, calls=%fused_computation.10.clone.1 | convolution fusion | flops 547356672 | bytes 10768896 | tf_op jit(solution)/shard_map/while/body/eval_jaxpr/kgnm,mkd->nkgd/dot_general | solution.py:53
  94.8 0.8 copy_dynamic-update-slice_fusion.2
  95.9 3.0 bitcast_reduce_fusion.2
  98.9 2.2 fusion.100
  101.1 1.0 copy-done.2
  102.3 5.7 %fusion.99 = bf16[4,128,8,32]{1,3,2,0:T(8,128)(2,1)S(1)} fusion(f32[4,2048,32,8]{1,2,3,0:T(8,128)} %copy-done.2, f32[4,8,32]{2,1,0:T(8,128)S(1)} %get-tuple-element.180, pred[2048]{0:T(1024)(128)(4,1)S(1)} %dynamic-slice_reduce_fusion.2, bf16[4,2048,4,128]{3,1,2,0:T(8,128)(2,1)} %get-tuple-element.205, s32[]{:T(128)} %get-tuple-element.191), kind=kOutput, calls=%fused_computation.10.clone.1 | convolution fusion | flops 547356672 | bytes 10768896 | tf_op jit(solution)/shard_map/while/body/eval_jaxpr/kgnm,mkd->nkgd/dot_general | solution.py:53
  108.0 0.8 copy_dynamic-update-slice_fusion.2
  109.1 3.0 bitcast_reduce_fusion.2
  112.1 2.2 fusion.100
  114.3 1.0 copy-done.2
  115.5 5.7 %fusion.99 = bf16[4,128,8,32]{1,3,2,0:T(8,128)(2,1)S(1)} fusion(f32[4,2048,32,8]{1,2,3,0:T(8,128)} %copy-done.2, f32[4,8,32]{2,1,0:T(8,128)S(1)} %get-tuple-element.180, pred[2048]{0:T(1024)(128)(4,1)S(1)} %dynamic-slice_reduce_fusion.2, bf16[4,2048,4,128]{3,1,2,0:T(8,128)(2,1)} %get-tuple-element.205, s32[]{:T(128)} %get-tuple-element.191), kind=kOutput, calls=%fused_computation.10.clone.1 | convolution fusion | flops 547356672 | bytes 10768896 | tf_op jit(solution)/shard_map/while/body/eval_jaxpr/kgnm,mkd->nkgd/dot_general | solution.py:53
  121.3 0.8 copy_dynamic-update-slice_fusion.2
  123.0 4.5 %all-to-all-start.2 = ((bf16[16,2,128]{2,1,0:T(2,128)(2,1)}), bf16[16,2,128]{2,1,0:T(2,128)(2,1)S(1)}, u32[]{:S(2)}, u32[]{:S(2)}) async-start(bf16[16,2,128]{2,1,0:T(2,128)(2,1)} %reshape.230), calls=%async_computation.2 | async-start | bytes 16384 | tf_op jit(solution)/shard_map/all_to_all | solution.py:174
  127.6 7.1 %all-to-all-done.2 = bf16[16,2,128]{2,1,0:T(2,128)(2,1)S(1)} async-done(((bf16[16,2,128]{2,1,0:T(2,128)(2,1)}), bf16[16,2,128]{2,1,0:T(2,128)(2,1)S(1)}, u32[]{:S(2)}, u32[]{:S(2)}) %all-to-all-start.2) | async-done | bytes 8224 | tf_op jit(solution)/shard_map/all_to_all | solution.py:174
  134.7 9.9 %all_to_all.33 = bf16[16,2,128]{2,1,0:T(2,128)(2,1)S(1)} all-to-all(bf16[16,2,128]{2,1,0:T(2,128)(2,1)S(1)} %reshape.228), channel_id=1, replica_groups=mesh['groups'=1,'ctx'=16,'tp'=2] {'ctx'}, dimensions={0} | all-to-all | bytes 16384 | tf_op jit(solution)/shard_map/all_to_all | solution.py:167
  144.6 3.7 %all-to-all-start = ((bf16[4,32,1,32,128]{4,3,0,2,1:T(8,128)(2,1)}), bf16[4,32,1,32,128]{4,3,0,2,1:T(8,128)(2,1)S(1)}, u32[]{:S(2)}, u32[]{:S(2)}) async-start(bf16[4,32,1,32,128]{4,3,0,2,1:T(8,128)(2,1)} %bitcast.237), calls=%async_computation | async-start | bytes 2097152 | tf_op jit(solution)/shard_map/all_to_all | solution.py:160
  148.3 47.7 %all_gather.10 = bf16[4,32,4,128]{3,2,0,1:T(4,128)(2,1)S(1)} all-gather(bf16[4,2,4,128]{3,2,0,1:T(4,128)(2,1)S(1)} %copy.90), channel_id=1, replica_groups=mesh['groups'=1,'ctx'=16,'tp'=2] {'ctx'}, dimensions={1}, use_global_device_ids=true | all-gather | bytes 139264 | tf_op jit(solution)/shard_map/all_gather | solution.py:131
  196.8 38.1 %all_gather.11 = bf16[4,32,4,128]{3,2,0,1:T(4,128)(2,1)S(1)} all-gather(bf16[4,2,4,128]{3,2,0,1:T(4,128)(2,1)S(1)} %copy.96), channel_id=1, replica_groups=mesh['groups'=1,'ctx'=16,'tp'=2] {'ctx'}, dimensions={1}, use_global_device_ids=true | all-gather | bytes 139264 | tf_op jit(solution)/shard_map/all_gather | solution.py:132
  235.5 1.5 copy.89
  237.0 0.7 copy.94
  238.0 0.7 mul.81
  239.0 3.9 %fusion.52 = f32[4,2,32,128]{3,1,2,0:T(2,128)S(1)} fusion(f32[4,16,2,1,32,128]{5,4,0,2,1,3:T(8,128)S(1)} %convert.23, f32[4,2,16,32]{1,2,3,0:T(8,128)} %copy.89), kind=kLoop, calls=%fused_computation.62 | loop fusion | flops 1015808 | bytes 2244608 | tf_op jit(solution)/shard_map/reduce_sum | solution.py:79
  243.6 7.7 %collective-permute-done = bf16[4,2,4096]{2,0,1:T(4,128)(2,1)S(1)} collective-permute-done((bf16[4,2,4096]{2,0,1:T(4,128)(2,1)S(1)}, bf16[4,2,4096]{2,0,1:T(4,128)(2,1)S(1)}, u32[]{:S(2)}, u32[]{:S(2)}) %collective-permute-start) | collective-permute-done | bytes 65568 | tf_op jit(solution)/shard_map/ppermute | solution.py:22
  251.3 5.6 %collective-permute-start.8 = (bf16[4,2,4096]{2,0,1:T(4,128)(2,1)S(1)}, bf16[4,2,4096]{2,0,1:T(4,128)(2,1)S(1)}, u32[]{:S(2)}, u32[]{:S(2)}) collective-permute-start(bf16[4,2,4096]{2,0,1:T(4,128)(2,1)S(1)} %fusion.57), channel_id=1, source_target_pairs={{0,30},{2,0},{4,2},{6,4},{8,6},{10,8},{12,10},{14,12},{16,14},{18,... | collective-permute-start | bytes 196616 | tf_op jit(solution)/shard_map/ppermute | solution.py:25
  256.9 2.5 collective-permute-done.1
  259.4 5.6 %collective-permute-start.9 = (bf16[4,2,4096]{2,0,1:T(4,128)(2,1)S(1)}, bf16[4,2,4096]{2,0,1:T(4,128)(2,1)S(1)}, u32[]{:S(2)}, u32[]{:S(2)}) collective-permute-start(bf16[4,2,4096]{2,0,1:T(4,128)(2,1)S(1)} %collective-permute-done.8), channel_id=1, source_target_pairs={{0,30},{2,0},{4,2},{6,4},{8,6},{10,8},{12,10},{14,12},{16,14},{18,... | collective-permute-start | bytes 196616 | tf_op jit(solution)/shard_map/ppermute | solution.py:25
  265.0 2.2 collective-permute-done.2
  267.3 5.6 %collective-permute-start.10 = (bf16[4,2,4096]{2,0,1:T(4,128)(2,1)S(1)}, bf16[4,2,4096]{2,0,1:T(4,128)(2,1)S(1)}, u32[]{:S(2)}, u32[]{:S(2)}) collective-permute-start(bf16[4,2,4096]{2,0,1:T(4,128)(2,1)S(1)} %collective-permute-done.9), channel_id=1, source_target_pairs={{0,30},{2,0},{4,2},{6,4},{8,6},{10,8},{12,10},{14,12},{16,14},{18,... | collective-permute-start | bytes 196616 | tf_op jit(solution)/shard_map/ppermute | solution.py:25
  272.9 2.2 collective-permute-done.3
  275.1 5.6 %collective-permute-start.11 = (bf16[4,2,4096]{2,0,1:T(4,128)(2,1)S(1)}, bf16[4,2,4096]{2,0,1:T(4,128)(2,1)S(1)}, u32[]{:S(2)}, u32[]{:S(2)}) collective-permute-start(bf16[4,2,4096]{2,0,1:T(4,128)(2,1)S(1)} %collective-permute-done.10), channel_id=1, source_target_pairs={{0,30},{2,0},{4,2},{6,4},{8,6},{10,8},{12,10},{14,12},{16,14},{18,... | collective-permute-start | bytes 196616 | tf_op jit(solution)/shard_map/ppermute | solution.py:25
  280.8 2.2 collective-permute-done.4
  283.0 5.6 %collective-permute-start.12 = (bf16[4,2,4096]{2,0,1:T(4,128)(2,1)S(1)}, bf16[4,2,4096]{2,0,1:T(4,128)(2,1)S(1)}, u32[]{:S(2)}, u32[]{:S(2)}) collective-permute-start(bf16[4,2,4096]{2,0,1:T(4,128)(2,1)S(1)} %collective-permute-done.11), channel_id=1, source_target_pairs={{0,30},{2,0},{4,2},{6,4},{8,6},{10,8},{12,10},{14,12},{16,14},{18,... | collective-permute-start | bytes 196616 | tf_op jit(solution)/shard_map/ppermute | solution.py:25
  288.6 2.2 collective-permute-done.5
  290.9 5.6 %collective-permute-start.13 = (bf16[4,2,4096]{2,0,1:T(4,128)(2,1)S(1)}, bf16[4,2,4096]{2,0,1:T(4,128)(2,1)S(1)}, u32[]{:S(2)}, u32[]{:S(2)}) collective-permute-start(bf16[4,2,4096]{2,0,1:T(4,128)(2,1)S(1)} %collective-permute-done.12), channel_id=1, source_target_pairs={{0,30},{2,0},{4,2},{6,4},{8,6},{10,8},{12,10},{14,12},{16,14},{18,... | collective-permute-start | bytes 196616 | tf_op jit(solution)/shard_map/ppermute | solution.py:25
  296.5 2.2 collective-permute-done.6
  298.7 5.6 %collective-permute-start.14 = (bf16[4,2,4096]{2,0,1:T(4,128)(2,1)S(1)}, bf16[4,2,4096]{2,0,1:T(4,128)(2,1)S(1)}, u32[]{:S(2)}, u32[]{:S(2)}) collective-permute-start(bf16[4,2,4096]{2,0,1:T(4,128)(2,1)S(1)} %collective-permute-done.13), channel_id=1, source_target_pairs={{0,30},{2,0},{4,2},{6,4},{8,6},{10,8},{12,10},{14,12},{16,14},{18,... | collective-permute-start | bytes 196616 | tf_op jit(solution)/shard_map/ppermute | solution.py:25
  304.4 2.2 collective-permute-done.7
  306.6 2.9 constant_dynamic-update-slice_fusion.31
  310.9 0.7 constant_dynamic-update-slice_fusion.28
  312.3 0.7 constant_dynamic-update-slice_fusion.26
  313.7 0.7 constant_dynamic-update-slice_fusion.24
  315.1 0.7 constant_dynamic-update-slice_fusion.22
  316.5 0.7 constant_dynamic-update-slice_fusion.20
  317.9 0.7 constant_dynamic-update-slice_fusion.18
  320.3 0.7 dynamic-slice_convert_fusion
  322.3 12.7 %all-reduce.3.cloned.1.call-done = bf16[4,32,512]{2,0,1:T(4,128)(2,1)} async-done(((bf16[4,32,512]{2,0,1:T(4,128)(2,1)}), bf16[4,32,512]{2,0,1:T(4,128)(2,1)}) %all-reduce.3.cloned.1.call-update) | async-done | bytes 131088
  334.9 0.9 constant_dynamic-slice_fusion
  (133 shorter events, 13.2 us)
Async XLA Ops:
  6.5 3.6 %copy-start = (bf16[16,128,4,128]{3,2,1,0:T(4,128)(2,1)S(1)}, bf16[16,128,4,128]{3,2,1,0:T(4,128)(2,1)}, u32[]{:S(2)}) copy-start(bf16[16,128,4,128]{3,2,1,0:T(4,128)(2,1)} %param.15) | copy-start | bytes 6291460
  6.5 61.2 %all-gather.2.cloned.1.call-start = ((), (), s32[]{:S(2)}) async-start(), calls=%async_computation.3 | async-start | bytes 1114112 | tf_op jit(solution)/shard_map/all_gather | solution.py:120
  69.4 78.9 %copy-start.6 = (bf16[4,2,4,128]{3,2,1,0:T(4,128)(2,1)S(1)}, bf16[4,2,4,128]{3,2,1,0:T(4,128)(2,1)}, u32[]{:S(2)}) copy-start(bf16[4,2,4,128]{3,2,1,0:T(4,128)(2,1)} %param.12) | copy-start | bytes 24580
  69.4 126.7 %copy-start.5 = (bf16[4,2,32,128]{3,2,1,0:T(8,128)(2,1)S(1)}, bf16[4,2,32,128]{3,2,1,0:T(8,128)(2,1)}, u32[]{:S(2)}) copy-start(bf16[4,2,32,128]{3,2,1,0:T(8,128)(2,1)} %param.11) | copy-start | bytes 196612
  69.4 127.4 %copy-start.7 = (bf16[4,2,4,128]{3,2,1,0:T(4,128)(2,1)S(1)}, bf16[4,2,4,128]{3,2,1,0:T(4,128)(2,1)}, u32[]{:S(2)}) copy-start(bf16[4,2,4,128]{3,2,1,0:T(4,128)(2,1)} %param.13) | copy-start | bytes 24580
  72.5 3.3 copy-start.2
  85.7 3.3 copy-start.2
  98.9 3.3 copy-start.2
  112.1 3.3 copy-start.2
  123.0 11.7 %all-to-all-start.2 = ((bf16[16,2,128]{2,1,0:T(2,128)(2,1)}), bf16[16,2,128]{2,1,0:T(2,128)(2,1)S(1)}, u32[]{:S(2)}, u32[]{:S(2)}) async-start(bf16[16,2,128]{2,1,0:T(2,128)(2,1)} %reshape.230), calls=%async_computation.2 | async-start | bytes 16384 | tf_op jit(solution)/shard_map/all_to_all | solution.py:174
  144.6 94.1 %all-to-all-start = ((bf16[4,32,1,32,128]{4,3,0,2,1:T(8,128)(2,1)}), bf16[4,32,1,32,128]{4,3,0,2,1:T(8,128)(2,1)S(1)}, u32[]{:S(2)}, u32[]{:S(2)}) async-start(bf16[4,32,1,32,128]{4,3,0,2,1:T(8,128)(2,1)} %bitcast.237), calls=%async_computation | async-start | bytes 2097152 | tf_op jit(solution)/shard_map/all_to_all | solution.py:160
  148.2 186.7 %all-reduce.3.cloned.1.call-start = ((), (), s32[]{:S(2)}) async-start(), calls=%async_computation.4 | async-start | bytes 262144
  238.7 4.5 %copy-start.3 = (f32[4,2,4096]{2,0,1:T(4,128)S(1)}, f32[4,2,4096]{2,0,1:T(4,128)}, u32[]{:S(2)}) copy-start(f32[4,2,4096]{2,0,1:T(4,128)} %mul.81) | copy-start | bytes 393220
  238.7 4.2 %copy-start.4 = (f32[4,2,32]{1,2,0:T(8,128)S(1)}, f32[4,2,32]{1,2,0:T(8,128)}, u32[]{:S(2)}) copy-start(f32[4,2,32]{1,2,0:T(8,128)} %copy.94) | copy-start | bytes 3076
  243.3 8.0 %collective-permute-start = (bf16[4,2,4096]{2,0,1:T(4,128)(2,1)S(1)}, bf16[4,2,4096]{2,0,1:T(4,128)(2,1)S(1)}, u32[]{:S(2)}, u32[]{:S(2)}) collective-permute-start(bf16[4,2,4096]{2,0,1:T(4,128)(2,1)S(1)} %fusion.57), channel_id=1, source_target_pairs={{0,2},{2,4},{4,6},{6,8},{8,10},{10,12},{12,14},{14,16},{16,18},{18... | collective-permute-start | bytes 196616 | tf_op jit(solution)/shard_map/ppermute | solution.py:22
  251.3 8.1 %collective-permute-start.1 = (bf16[4,2,4096]{2,0,1:T(4,128)(2,1)S(1)}, bf16[4,2,4096]{2,0,1:T(4,128)(2,1)S(1)}, u32[]{:S(2)}, u32[]{:S(2)}) collective-permute-start(bf16[4,2,4096]{2,0,1:T(4,128)(2,1)S(1)} %collective-permute-done), channel_id=1, source_target_pairs={{0,2},{2,4},{4,6},{6,8},{8,10},{10,12},{12,14},{14,16},{16,18},{18... | collective-permute-start | bytes 196616 | tf_op jit(solution)/shard_map/ppermute | solution.py:22
  251.3 8.1 %collective-permute-start.8 = (bf16[4,2,4096]{2,0,1:T(4,128)(2,1)S(1)}, bf16[4,2,4096]{2,0,1:T(4,128)(2,1)S(1)}, u32[]{:S(2)}, u32[]{:S(2)}) collective-permute-start(bf16[4,2,4096]{2,0,1:T(4,128)(2,1)S(1)} %fusion.57), channel_id=1, source_target_pairs={{0,30},{2,0},{4,2},{6,4},{8,6},{10,8},{12,10},{14,12},{16,14},{18,... | collective-permute-start | bytes 196616 | tf_op jit(solution)/shard_map/ppermute | solution.py:25
  259.4 7.9 %collective-permute-start.2 = (bf16[4,2,4096]{2,0,1:T(4,128)(2,1)S(1)}, bf16[4,2,4096]{2,0,1:T(4,128)(2,1)S(1)}, u32[]{:S(2)}, u32[]{:S(2)}) collective-permute-start(bf16[4,2,4096]{2,0,1:T(4,128)(2,1)S(1)} %collective-permute-done.1), channel_id=1, source_target_pairs={{0,2},{2,4},{4,6},{6,8},{8,10},{10,12},{12,14},{14,16},{16,18},{18... | collective-permute-start | bytes 196616 | tf_op jit(solution)/shard_map/ppermute | solution.py:22
  259.4 7.9 %collective-permute-start.9 = (bf16[4,2,4096]{2,0,1:T(4,128)(2,1)S(1)}, bf16[4,2,4096]{2,0,1:T(4,128)(2,1)S(1)}, u32[]{:S(2)}, u32[]{:S(2)}) collective-permute-start(bf16[4,2,4096]{2,0,1:T(4,128)(2,1)S(1)} %collective-permute-done.8), channel_id=1, source_target_pairs={{0,30},{2,0},{4,2},{6,4},{8,6},{10,8},{12,10},{14,12},{16,14},{18,... | collective-permute-start | bytes 196616 | tf_op jit(solution)/shard_map/ppermute | solution.py:25
  267.3 7.9 %collective-permute-start.3 = (bf16[4,2,4096]{2,0,1:T(4,128)(2,1)S(1)}, bf16[4,2,4096]{2,0,1:T(4,128)(2,1)S(1)}, u32[]{:S(2)}, u32[]{:S(2)}) collective-permute-start(bf16[4,2,4096]{2,0,1:T(4,128)(2,1)S(1)} %collective-permute-done.2), channel_id=1, source_target_pairs={{0,2},{2,4},{4,6},{6,8},{8,10},{10,12},{12,14},{14,16},{16,18},{18... | collective-permute-start | bytes 196616 | tf_op jit(solution)/shard_map/ppermute | solution.py:22
  267.3 7.9 %collective-permute-start.10 = (bf16[4,2,4096]{2,0,1:T(4,128)(2,1)S(1)}, bf16[4,2,4096]{2,0,1:T(4,128)(2,1)S(1)}, u32[]{:S(2)}, u32[]{:S(2)}) collective-permute-start(bf16[4,2,4096]{2,0,1:T(4,128)(2,1)S(1)} %collective-permute-done.9), channel_id=1, source_target_pairs={{0,30},{2,0},{4,2},{6,4},{8,6},{10,8},{12,10},{14,12},{16,14},{18,... | collective-permute-start | bytes 196616 | tf_op jit(solution)/shard_map/ppermute | solution.py:25
  275.1 7.9 %collective-permute-start.4 = (bf16[4,2,4096]{2,0,1:T(4,128)(2,1)S(1)}, bf16[4,2,4096]{2,0,1:T(4,128)(2,1)S(1)}, u32[]{:S(2)}, u32[]{:S(2)}) collective-permute-start(bf16[4,2,4096]{2,0,1:T(4,128)(2,1)S(1)} %collective-permute-done.3), channel_id=1, source_target_pairs={{0,2},{2,4},{4,6},{6,8},{8,10},{10,12},{12,14},{14,16},{16,18},{18... | collective-permute-start | bytes 196616 | tf_op jit(solution)/shard_map/ppermute | solution.py:22
  275.1 7.9 %collective-permute-start.11 = (bf16[4,2,4096]{2,0,1:T(4,128)(2,1)S(1)}, bf16[4,2,4096]{2,0,1:T(4,128)(2,1)S(1)}, u32[]{:S(2)}, u32[]{:S(2)}) collective-permute-start(bf16[4,2,4096]{2,0,1:T(4,128)(2,1)S(1)} %collective-permute-done.10), channel_id=1, source_target_pairs={{0,30},{2,0},{4,2},{6,4},{8,6},{10,8},{12,10},{14,12},{16,14},{18,... | collective-permute-start | bytes 196616 | tf_op jit(solution)/shard_map/ppermute | solution.py:25
  283.0 7.9 %collective-permute-start.5 = (bf16[4,2,4096]{2,0,1:T(4,128)(2,1)S(1)}, bf16[4,2,4096]{2,0,1:T(4,128)(2,1)S(1)}, u32[]{:S(2)}, u32[]{:S(2)}) collective-permute-start(bf16[4,2,4096]{2,0,1:T(4,128)(2,1)S(1)} %collective-permute-done.4), channel_id=1, source_target_pairs={{0,2},{2,4},{4,6},{6,8},{8,10},{10,12},{12,14},{14,16},{16,18},{18... | collective-permute-start | bytes 196616 | tf_op jit(solution)/shard_map/ppermute | solution.py:22
  283.0 7.9 %collective-permute-start.12 = (bf16[4,2,4096]{2,0,1:T(4,128)(2,1)S(1)}, bf16[4,2,4096]{2,0,1:T(4,128)(2,1)S(1)}, u32[]{:S(2)}, u32[]{:S(2)}) collective-permute-start(bf16[4,2,4096]{2,0,1:T(4,128)(2,1)S(1)} %collective-permute-done.11), channel_id=1, source_target_pairs={{0,30},{2,0},{4,2},{6,4},{8,6},{10,8},{12,10},{14,12},{16,14},{18,... | collective-permute-start | bytes 196616 | tf_op jit(solution)/shard_map/ppermute | solution.py:25
  290.9 7.9 %collective-permute-start.6 = (bf16[4,2,4096]{2,0,1:T(4,128)(2,1)S(1)}, bf16[4,2,4096]{2,0,1:T(4,128)(2,1)S(1)}, u32[]{:S(2)}, u32[]{:S(2)}) collective-permute-start(bf16[4,2,4096]{2,0,1:T(4,128)(2,1)S(1)} %collective-permute-done.5), channel_id=1, source_target_pairs={{0,2},{2,4},{4,6},{6,8},{8,10},{10,12},{12,14},{14,16},{16,18},{18... | collective-permute-start | bytes 196616 | tf_op jit(solution)/shard_map/ppermute | solution.py:22
  290.9 7.9 %collective-permute-start.13 = (bf16[4,2,4096]{2,0,1:T(4,128)(2,1)S(1)}, bf16[4,2,4096]{2,0,1:T(4,128)(2,1)S(1)}, u32[]{:S(2)}, u32[]{:S(2)}) collective-permute-start(bf16[4,2,4096]{2,0,1:T(4,128)(2,1)S(1)} %collective-permute-done.12), channel_id=1, source_target_pairs={{0,30},{2,0},{4,2},{6,4},{8,6},{10,8},{12,10},{14,12},{16,14},{18,... | collective-permute-start | bytes 196616 | tf_op jit(solution)/shard_map/ppermute | solution.py:25
  298.7 7.9 %collective-permute-start.7 = (bf16[4,2,4096]{2,0,1:T(4,128)(2,1)S(1)}, bf16[4,2,4096]{2,0,1:T(4,128)(2,1)S(1)}, u32[]{:S(2)}, u32[]{:S(2)}) collective-permute-start(bf16[4,2,4096]{2,0,1:T(4,128)(2,1)S(1)} %collective-permute-done.6), channel_id=1, source_target_pairs={{0,2},{2,4},{4,6},{6,8},{8,10},{10,12},{12,14},{14,16},{16,18},{18... | collective-permute-start | bytes 196616 | tf_op jit(solution)/shard_map/ppermute | solution.py:22
  298.7 10.7 %copy-start.1 = (bf16[4096,512]{1,0:T(8,128)(2,1)S(1)}, bf16[4096,512]{1,0:T(8,128)(2,1)}, u32[]{:S(2)}) copy-start(bf16[4096,512]{1,0:T(8,128)(2,1)} %param.17) | copy-start | bytes 12582916
  298.7 20.6 %collective-permute-start.14 = (bf16[4,2,4096]{2,0,1:T(4,128)(2,1)S(1)}, bf16[4,2,4096]{2,0,1:T(4,128)(2,1)S(1)}, u32[]{:S(2)}, u32[]{:S(2)}) collective-permute-start(bf16[4,2,4096]{2,0,1:T(4,128)(2,1)S(1)} %collective-permute-done.13), channel_id=1, source_target_pairs={{0,30},{2,0},{4,2},{6,4},{8,6},{10,8},{12,10},{14,12},{16,14},{18,... | collective-permute-start | bytes 196616 | tf_op jit(solution)/shard_map/ppermute | solution.py:25
  319.3 1.7 copy-start.8
Sparse Core Ops, SparseCore 0:
  10.1 57.6 all-gather.1
  321.1 13.7 all-reduce.2
